TPU v7x, 512 devices: a whole 4x8x8 slice. The times are simulated.
512 devices in a mesh: tm: 512 (over x, z, y, core).
Axes of the slice: x: 4, y: 8, z: 8, core: 2. Of those that a mesh axis runs over, the one named last changes fastest.
Arguments:
- inv_diag: float32 [512, 384, 384], P('tm'), may hold values from -0.4 to 4.4, as said below
- low_coupling: float32 [512, 384, 384], P('tm'), may hold values from -0.09375 to 0.09375
- up_coupling: float32 [512, 384, 384], P('tm'), may hold values from -0.09375 to 0.09375
Outputs:
- diag_inverse: float32 [512, 384, 384], P('tm')
- cross_inverse: float32 [512, 384, 384], P('tm')
Inputs may be any that keep to these rules, and one draw needn't show every extreme that they name: `inv_diag`: each block is symmetric.
All inputs are finite; a program needn't handle non-finite values.
Results may differ from a plain program's by a relative error of at most 0.00012.
Values sent between devices are 32-bit elements; how exact they have to be, the bound alone decides.
A program may use at most 64 MiB of HBM per device.

v0:
```python
import jax
import jax.numpy as jnp
from jax import lax
from jax.sharding import PartitionSpec as P

row_offset = 3


def passed_along(array, axis, by):
    peers = lax.axis_size(axis)
    return lax.ppermute(array, axis, [(i, (i + by) % peers) for i in range(peers)])


def product(left, right):
    return jnp.dot(left, right, precision=lax.Precision.HIGHEST, preferred_element_type=jnp.float32)


def body(inv_diag, low_coupling, up_coupling):
    inverse = inv_diag[0]
    lowers = low_coupling[0]
    uppers = up_coupling[0]
    width = inverse.shape[0]
    length = lax.axis_size("tm")
    levels = length.bit_length() - 1
    place = lax.axis_index("tm")
    position = (place + row_offset) % length
    zeros = jnp.zeros((width, width), jnp.float32)
    sigma = jnp.where(position == 0, inverse, zeros)
    high_own = zeros
    low_own = zeros
    lower_cross = zeros
    g_mat = product(inverse, lowers)
    h_mat = product(inverse, uppers)

    def eliminate(operands):
        current, sigma_low, sigma_high, sigma_ba = operands
        sigma_ab = sigma_ba.T
        part_low = -(product(g_mat, sigma_low) + product(h_mat, sigma_ba))
        part_high = -(product(g_mat, sigma_ab) + product(h_mat, sigma_high))
        sigma_tt = inverse - product(g_mat, part_low.T) - product(h_mat, part_high.T)
        return (sigma_tt, part_low, part_high)

    def keep(operands):
        return (operands[0], zeros, zeros)

    for step_num in range(levels):
        stride = length // 2 ** (step_num + 1)
        active = position % (2 * stride) == stride
        has_upper = position + stride < length
        from_low, owned_high = passed_along((sigma, high_own), "tm", stride)
        from_high, owned_low = passed_along((sigma, low_own), "tm", -stride)
        sigma_ba = owned_high.T + owned_low
        sigma_high = jnp.where(has_upper, from_high, zeros)
        sigma_ba = jnp.where(has_upper, sigma_ba, zeros)
        sigma, part_low, part_high = lax.cond(
            active, eliminate, keep, (sigma, from_low, sigma_high, sigma_ba)
        )
        high_own = part_high
        low_own = part_low
        lower_cross = jnp.where(active, part_low, lower_cross)
    return (sigma[None], lower_cross[None])


def solution(mesh):
    placed = (P("tm", None, None), P("tm", None, None), P("tm", None, None))
    return jax.shard_map(
        body,
        mesh=mesh,
        in_specs=placed,
        out_specs=(P("tm", None, None), P("tm", None, None)),
        check_vma=False,
    )
```

profile of v0, /device:TPU:4, one launch (start us, length us, event | category | flops | bytes accessed | tf_op | source)
XLA Modules:
  0.0 573.9 jit_solution(7740354289249144527)
XLA Ops:
  0.7 7.9 %collective-permute-start.1 = (f32[384,384]{1,0:T(8,128)S(1)}, f32[384,384]{1,0:T(8,128)S(1)}, u32[]{:S(2)}, u32[]{:S(2)}) collective-permute-start(f32[384,384]{1,0:T(8,128)S(1)} %broadcast_in_dim.36), channel_id=1, source_target_pairs={{0,256},{1,257},{2,258},{3,259},{4,260},{5,261},{6,262},{7,263},{8... | collective-permute-start | bytes 1769480 | tf_op jit(solution)/shard_map/ppermute | solution.py:11
  14.0 8.8 %collective-permute-done.1 = f32[384,384]{1,0:T(8,128)S(1)} collective-permute-done((f32[384,384]{1,0:T(8,128)S(1)}, f32[384,384]{1,0:T(8,128)S(1)}, u32[]{:S(2)}, u32[]{:S(2)}) %collective-permute-start.1) | collective-permute-done | bytes 589856 | tf_op jit(solution)/shard_map/ppermute | solution.py:11
  22.8 9.2 %collective-permute-done = f32[384,384]{1,0:T(8,128)S(1)} collective-permute-done((f32[384,384]{1,0:T(8,128)}, f32[384,384]{1,0:T(8,128)S(1)}, u32[]{:S(2)}, u32[]{:S(2)}) %collective-permute-start) | collective-permute-done | bytes 589856 | tf_op jit(solution)/shard_map/ppermute | solution.py:11
  57.0 10.3 %collective-permute-done.3 = f32[384,384]{0,1:T(8,128)S(1)} collective-permute-done((f32[384,384]{0,1:T(8,128)}, f32[384,384]{0,1:T(8,128)S(1)}, u32[]{:S(2)}, u32[]{:S(2)}) %collective-permute-start.3) | collective-permute-done | bytes 589856 | tf_op jit(solution)/shard_map/ppermute | solution.py:11
  69.5 11.9 %collective-permute-start.9 = (f32[384,384]{1,0:T(8,128)}, f32[384,384]{1,0:T(8,128)}, u32[]{:S(2)}, u32[]{:S(2)}) collective-permute-start(f32[384,384]{1,0:T(8,128)} %copy.28), channel_id=1, source_target_pairs={{0,448},{1,449},{2,450},{3,451},{4,452},{5,453},{6,454},{7,455},{8... | collective-permute-start | bytes 1769480 | tf_op jit(solution)/shard_map/ppermute | solution.py:11
  95.4 13.2 %collective-permute-done.6 = f32[384,384]{1,0:T(8,128)} collective-permute-done((f32[384,384]{1,0:T(8,128)}, f32[384,384]{1,0:T(8,128)}, u32[]{:S(2)}, u32[]{:S(2)}) %collective-permute-start.6) | collective-permute-done | bytes 589856 | tf_op jit(solution)/shard_map/ppermute | solution.py:11
  108.6 12.6 %collective-permute-done.7 = f32[384,384]{0,1:T(8,128)} collective-permute-done((f32[384,384]{0,1:T(8,128)}, f32[384,384]{0,1:T(8,128)}, u32[]{:S(2)}, u32[]{:S(2)}) %collective-permute-start.7) | collective-permute-done | bytes 589856 | tf_op jit(solution)/shard_map/ppermute | solution.py:11
  121.3 59.5 %collective-permute-done.8 = f32[384,384]{1,0:T(8,128)} collective-permute-done((f32[384,384]{1,0:T(8,128)S(1)}, f32[384,384]{1,0:T(8,128)}, u32[]{:S(2)}, u32[]{:S(2)}) %collective-permute-start.8) | collective-permute-done | bytes 589856 | tf_op jit(solution)/shard_map/ppermute | solution.py:11
  184.0 8.2 %collective-permute-start.13 = (f32[384,384]{1,0:T(8,128)}, f32[384,384]{1,0:T(8,128)}, u32[]{:S(2)}, u32[]{:S(2)}) collective-permute-start(f32[384,384]{1,0:T(8,128)} %copy.31), channel_id=1, source_target_pairs={{0,480},{1,481},{2,482},{3,483},{4,484},{5,485},{6,486},{7,487},{8... | collective-permute-start | bytes 1769480 | tf_op jit(solution)/shard_map/ppermute | solution.py:11
  202.9 24.3 %collective-permute-done.13 = f32[384,384]{1,0:T(8,128)} collective-permute-done((f32[384,384]{1,0:T(8,128)}, f32[384,384]{1,0:T(8,128)}, u32[]{:S(2)}, u32[]{:S(2)}) %collective-permute-start.13) | collective-permute-done | bytes 589856 | tf_op jit(solution)/shard_map/ppermute | solution.py:11
  234.2 12.5 %collective-permute-done.11 = f32[384,384]{0,1:T(8,128)} collective-permute-done((f32[384,384]{0,1:T(8,128)}, f32[384,384]{0,1:T(8,128)}, u32[]{:S(2)}, u32[]{:S(2)}) %collective-permute-start.11) | collective-permute-done | bytes 589856 | tf_op jit(solution)/shard_map/ppermute | solution.py:11
  272.2 11.7 %collective-permute-done.15 = f32[384,384]{0,1:T(8,128)} collective-permute-done((f32[384,384]{0,1:T(8,128)}, f32[384,384]{0,1:T(8,128)}, u32[]{:S(2)}, u32[]{:S(2)}) %collective-permute-start.15) | collective-permute-done | bytes 589856 | tf_op jit(solution)/shard_map/ppermute | solution.py:11
  296.6 8.6 %collective-permute-start.19 = (f32[384,384]{0,1:T(8,128)}, f32[384,384]{0,1:T(8,128)}, u32[]{:S(2)}, u32[]{:S(2)}) collective-permute-start(f32[384,384]{0,1:T(8,128)} %get-tuple-element.551), channel_id=1, source_target_pairs={{0,8},{1,9},{2,10},{3,11},{4,12},{5,13},{6,14},{7,15},{8,16},{9,17... | collective-permute-start | bytes 1769480 | tf_op jit(solution)/shard_map/ppermute | solution.py:11
  309.4 26.9 %collective-permute-done.18 = f32[384,384]{1,0:T(8,128)} collective-permute-done((f32[384,384]{1,0:T(8,128)}, f32[384,384]{1,0:T(8,128)}, u32[]{:S(2)}, u32[]{:S(2)}) %collective-permute-start.18) | collective-permute-done | bytes 589856 | tf_op jit(solution)/shard_map/ppermute | solution.py:11
  336.3 25.2 %collective-permute-done.19 = f32[384,384]{0,1:T(8,128)} collective-permute-done((f32[384,384]{0,1:T(8,128)}, f32[384,384]{0,1:T(8,128)}, u32[]{:S(2)}, u32[]{:S(2)}) %collective-permute-start.19) | collective-permute-done | bytes 589856 | tf_op jit(solution)/shard_map/ppermute | solution.py:11
  364.7 43.9 %collective-permute-start.25 = (f32[384,384]{1,0:T(8,128)}, f32[384,384]{1,0:T(8,128)}, u32[]{:S(2)}, u32[]{:S(2)}) collective-permute-start(f32[384,384]{1,0:T(8,128)} %copy.40), channel_id=1, source_target_pairs={{0,508},{1,509},{2,510},{3,511},{4,0},{5,1},{6,2},{7,3},{8,4},{9,5... | collective-permute-start | bytes 1769480 | tf_op jit(solution)/shard_map/ppermute | solution.py:11
  412.4 9.0 %collective-permute-start.24 = (f32[384,384]{1,0:T(8,128)}, f32[384,384]{1,0:T(8,128)}, u32[]{:S(2)}, u32[]{:S(2)}) collective-permute-start(f32[384,384]{1,0:T(8,128)} %get-tuple-element.555), channel_id=1, source_target_pairs={{0,508},{1,509},{2,510},{3,511},{4,0},{5,1},{6,2},{7,3},{8,4},{9,5... | collective-permute-start | bytes 1769480 | tf_op jit(solution)/shard_map/ppermute | solution.py:11
  421.5 20.2 %collective-permute-done.25 = f32[384,384]{1,0:T(8,128)} collective-permute-done((f32[384,384]{1,0:T(8,128)}, f32[384,384]{1,0:T(8,128)}, u32[]{:S(2)}, u32[]{:S(2)}) %collective-permute-start.25) | collective-permute-done | bytes 589856 | tf_op jit(solution)/shard_map/ppermute | solution.py:11
  441.7 12.5 %collective-permute-done.22 = f32[384,384]{1,0:T(8,128)} collective-permute-done((f32[384,384]{1,0:T(8,128)}, f32[384,384]{1,0:T(8,128)}, u32[]{:S(2)}, u32[]{:S(2)}) %collective-permute-start.22) | collective-permute-done | bytes 589856 | tf_op jit(solution)/shard_map/ppermute | solution.py:11
  454.3 12.5 %collective-permute-done.23 = f32[384,384]{0,1:T(8,128)} collective-permute-done((f32[384,384]{0,1:T(8,128)}, f32[384,384]{0,1:T(8,128)}, u32[]{:S(2)}, u32[]{:S(2)}) %collective-permute-start.23) | collective-permute-done | bytes 589856 | tf_op jit(solution)/shard_map/ppermute | solution.py:11
  477.5 8.1 %collective-permute-start.28 = (f32[384,384]{1,0:T(8,128)}, f32[384,384]{1,0:T(8,128)}, u32[]{:S(2)}, u32[]{:S(2)}) collective-permute-start(f32[384,384]{1,0:T(8,128)} %get-tuple-element.558), channel_id=1, source_target_pairs={{0,510},{1,511},{2,0},{3,1},{4,2},{5,3},{6,4},{7,5},{8,6},{9,7},{1... | collective-permute-start | bytes 1769480 | tf_op jit(solution)/shard_map/ppermute | solution.py:11
  502.4 30.0 %collective-permute-start.33 = (f32[384,384]{1,0:T(8,128)}, f32[384,384]{1,0:T(8,128)}, u32[]{:S(2)}, u32[]{:S(2)}) collective-permute-start(f32[384,384]{1,0:T(8,128)} %copy.46), channel_id=1, source_target_pairs={{0,511},{1,0},{2,1},{3,2},{4,3},{5,4},{6,5},{7,6},{8,7},{9,8},{10,... | collective-permute-start | bytes 1769480 | tf_op jit(solution)/shard_map/ppermute | solution.py:11
  536.3 7.9 %collective-permute-start.32 = (f32[384,384]{1,0:T(8,128)}, f32[384,384]{1,0:T(8,128)}, u32[]{:S(2)}, u32[]{:S(2)}) collective-permute-start(f32[384,384]{1,0:T(8,128)} %get-tuple-element.561), channel_id=1, source_target_pairs={{0,511},{1,0},{2,1},{3,2},{4,3},{5,4},{6,5},{7,6},{8,7},{9,8},{10,... | collective-permute-start | bytes 1769480 | tf_op jit(solution)/shard_map/ppermute | solution.py:11
  554.5 15.9 %conditional.17 = (f32[384,384]{0,1:T(8,128)S(1)}, f32[384,384]{1,0:T(8,128)}) conditional(s32[]{:T(128)} %convert_element_type.27, f32[384,384]{0,1:T(8,128)S(1)} %get-tuple-element.559, (f32[384,384]{1,0:T(8,128)S(1)}, f32[384,384]{1,0:T(8,128)}, s32[]{:T(128)}, f32[384,384]{1,0:T(8,128)}, f32[384,384]{1,0:T(8,128)}, ...), branch_computations={%region_16.17_spmd, %region_17.18_spmd} | conditional | flops 4078190592 | bytes 19464260 | solution.py:55
  (102 shorter events, 191.3 us)
Async XLA Ops:
  0.7 22.1 %collective-permute-start.1 = (f32[384,384]{1,0:T(8,128)S(1)}, f32[384,384]{1,0:T(8,128)S(1)}, u32[]{:S(2)}, u32[]{:S(2)}) collective-permute-start(f32[384,384]{1,0:T(8,128)S(1)} %broadcast_in_dim.36), channel_id=1, source_target_pairs={{0,256},{1,257},{2,258},{3,259},{4,260},{5,261},{6,262},{7,263},{8... | collective-permute-start | bytes 1769480 | tf_op jit(solution)/shard_map/ppermute | solution.py:11
  9.5 22.5 %collective-permute-start = (f32[384,384]{1,0:T(8,128)}, f32[384,384]{1,0:T(8,128)S(1)}, u32[]{:S(2)}, u32[]{:S(2)}) collective-permute-start(f32[384,384]{1,0:T(8,128)} %broadcast_select_fusion), channel_id=1, source_target_pairs={{0,256},{1,257},{2,258},{3,259},{4,260},{5,261},{6,262},{7,263},{8... | collective-permute-start | bytes 1769480 | tf_op jit(solution)/shard_map/ppermute | solution.py:11
  42.0 25.3 %collective-permute-start.3 = (f32[384,384]{0,1:T(8,128)}, f32[384,384]{0,1:T(8,128)S(1)}, u32[]{:S(2)}, u32[]{:S(2)}) collective-permute-start(f32[384,384]{0,1:T(8,128)} %get-tuple-element.539), channel_id=1, source_target_pairs={{0,128},{1,129},{2,130},{3,131},{4,132},{5,133},{6,134},{7,135},{8... | collective-permute-start | bytes 1769480 | tf_op jit(solution)/shard_map/ppermute | solution.py:11
  46.3 20.9 %collective-permute-start.4 = (f32[384,384]{1,0:T(8,128)}, f32[384,384]{1,0:T(8,128)}, u32[]{:S(2)}, u32[]{:S(2)}) collective-permute-start(f32[384,384]{1,0:T(8,128)} %get-tuple-element.540), channel_id=1, source_target_pairs={{0,384},{1,385},{2,386},{3,387},{4,388},{5,389},{6,390},{7,391},{8... | collective-permute-start | bytes 1769480 | tf_op jit(solution)/shard_map/ppermute | solution.py:11
  69.5 26.0 %collective-permute-start.9 = (f32[384,384]{1,0:T(8,128)}, f32[384,384]{1,0:T(8,128)}, u32[]{:S(2)}, u32[]{:S(2)}) collective-permute-start(f32[384,384]{1,0:T(8,128)} %copy.28), channel_id=1, source_target_pairs={{0,448},{1,449},{2,450},{3,451},{4,452},{5,453},{6,454},{7,455},{8... | collective-permute-start | bytes 1769480 | tf_op jit(solution)/shard_map/ppermute | solution.py:11
  81.4 27.3 %collective-permute-start.6 = (f32[384,384]{1,0:T(8,128)}, f32[384,384]{1,0:T(8,128)}, u32[]{:S(2)}, u32[]{:S(2)}) collective-permute-start(f32[384,384]{1,0:T(8,128)} %copy.28), channel_id=1, source_target_pairs={{0,64},{1,65},{2,66},{3,67},{4,68},{5,69},{6,70},{7,71},{8,72},{9,... | collective-permute-start | bytes 1769480 | tf_op jit(solution)/shard_map/ppermute | solution.py:11
  83.3 38.0 %collective-permute-start.7 = (f32[384,384]{0,1:T(8,128)}, f32[384,384]{0,1:T(8,128)}, u32[]{:S(2)}, u32[]{:S(2)}) collective-permute-start(f32[384,384]{0,1:T(8,128)} %get-tuple-element.542), channel_id=1, source_target_pairs={{0,64},{1,65},{2,66},{3,67},{4,68},{5,69},{6,70},{7,71},{8,72},{9,... | collective-permute-start | bytes 1769480 | tf_op jit(solution)/shard_map/ppermute | solution.py:11
  91.0 89.8 %collective-permute-start.8 = (f32[384,384]{1,0:T(8,128)S(1)}, f32[384,384]{1,0:T(8,128)}, u32[]{:S(2)}, u32[]{:S(2)}) collective-permute-start(f32[384,384]{1,0:T(8,128)S(1)} %get-tuple-element.543), channel_id=1, source_target_pairs={{0,448},{1,449},{2,450},{3,451},{4,452},{5,453},{6,454},{7,455},{8... | collective-permute-start | bytes 1769480 | tf_op jit(solution)/shard_map/ppermute | solution.py:11
  184.0 43.3 %collective-permute-start.13 = (f32[384,384]{1,0:T(8,128)}, f32[384,384]{1,0:T(8,128)}, u32[]{:S(2)}, u32[]{:S(2)}) collective-permute-start(f32[384,384]{1,0:T(8,128)} %copy.31), channel_id=1, source_target_pairs={{0,480},{1,481},{2,482},{3,483},{4,484},{5,485},{6,486},{7,487},{8... | collective-permute-start | bytes 1769480 | tf_op jit(solution)/shard_map/ppermute | solution.py:11
  192.1 42.1 %collective-permute-start.10 = (f32[384,384]{1,0:T(8,128)}, f32[384,384]{1,0:T(8,128)}, u32[]{:S(2)}, u32[]{:S(2)}) collective-permute-start(f32[384,384]{1,0:T(8,128)} %copy.31), channel_id=1, source_target_pairs={{0,32},{1,33},{2,34},{3,35},{4,36},{5,37},{6,38},{7,39},{8,40},{9,... | collective-permute-start | bytes 1769480 | tf_op jit(solution)/shard_map/ppermute | solution.py:11
  194.1 52.7 %collective-permute-start.11 = (f32[384,384]{0,1:T(8,128)}, f32[384,384]{0,1:T(8,128)}, u32[]{:S(2)}, u32[]{:S(2)}) collective-permute-start(f32[384,384]{0,1:T(8,128)} %get-tuple-element.545), channel_id=1, source_target_pairs={{0,32},{1,33},{2,34},{3,35},{4,36},{5,37},{6,38},{7,39},{8,40},{9,... | collective-permute-start | bytes 1769480 | tf_op jit(solution)/shard_map/ppermute | solution.py:11
  196.6 50.2 %collective-permute-start.12 = (f32[384,384]{1,0:T(8,128)}, f32[384,384]{1,0:T(8,128)}, u32[]{:S(2)}, u32[]{:S(2)}) collective-permute-start(f32[384,384]{1,0:T(8,128)} %get-tuple-element.546), channel_id=1, source_target_pairs={{0,480},{1,481},{2,482},{3,483},{4,484},{5,485},{6,486},{7,487},{8... | collective-permute-start | bytes 1769480 | tf_op jit(solution)/shard_map/ppermute | solution.py:11
  255.6 28.3 %collective-permute-start.15 = (f32[384,384]{0,1:T(8,128)}, f32[384,384]{0,1:T(8,128)}, u32[]{:S(2)}, u32[]{:S(2)}) collective-permute-start(f32[384,384]{0,1:T(8,128)} %get-tuple-element.548), channel_id=1, source_target_pairs={{0,16},{1,17},{2,18},{3,19},{4,20},{5,21},{6,22},{7,23},{8,24},{9,... | collective-permute-start | bytes 1769480 | tf_op jit(solution)/shard_map/ppermute | solution.py:11
  257.5 26.4 %collective-permute-start.16 = (f32[384,384]{1,0:T(8,128)}, f32[384,384]{1,0:T(8,128)}, u32[]{:S(2)}, u32[]{:S(2)}) collective-permute-start(f32[384,384]{1,0:T(8,128)} %get-tuple-element.549), channel_id=1, source_target_pairs={{0,496},{1,497},{2,498},{3,499},{4,500},{5,501},{6,502},{7,503},{8... | collective-permute-start | bytes 1769480 | tf_op jit(solution)/shard_map/ppermute | solution.py:11
  286.8 22.6 %collective-permute-start.21 = (f32[384,384]{1,0:T(8,128)}, f32[384,384]{1,0:T(8,128)}, u32[]{:S(2)}, u32[]{:S(2)}) collective-permute-start(f32[384,384]{1,0:T(8,128)} %copy.37), channel_id=1, source_target_pairs={{0,504},{1,505},{2,506},{3,507},{4,508},{5,509},{6,510},{7,511},{8... | collective-permute-start | bytes 1769480 | tf_op jit(solution)/shard_map/ppermute | solution.py:11
  293.6 42.8 %collective-permute-start.18 = (f32[384,384]{1,0:T(8,128)}, f32[384,384]{1,0:T(8,128)}, u32[]{:S(2)}, u32[]{:S(2)}) collective-permute-start(f32[384,384]{1,0:T(8,128)} %copy.37), channel_id=1, source_target_pairs={{0,8},{1,9},{2,10},{3,11},{4,12},{5,13},{6,14},{7,15},{8,16},{9,17... | collective-permute-start | bytes 1769480 | tf_op jit(solution)/shard_map/ppermute | solution.py:11
  296.6 64.9 %collective-permute-start.19 = (f32[384,384]{0,1:T(8,128)}, f32[384,384]{0,1:T(8,128)}, u32[]{:S(2)}, u32[]{:S(2)}) collective-permute-start(f32[384,384]{0,1:T(8,128)} %get-tuple-element.551), channel_id=1, source_target_pairs={{0,8},{1,9},{2,10},{3,11},{4,12},{5,13},{6,14},{7,15},{8,16},{9,17... | collective-permute-start | bytes 1769480 | tf_op jit(solution)/shard_map/ppermute | solution.py:11
  305.2 56.3 %collective-permute-start.20 = (f32[384,384]{1,0:T(8,128)}, f32[384,384]{1,0:T(8,128)}, u32[]{:S(2)}, u32[]{:S(2)}) collective-permute-start(f32[384,384]{1,0:T(8,128)} %get-tuple-element.552), channel_id=1, source_target_pairs={{0,504},{1,505},{2,506},{3,507},{4,508},{5,509},{6,510},{7,511},{8... | collective-permute-start | bytes 1769480 | tf_op jit(solution)/shard_map/ppermute | solution.py:11
  364.7 77.0 %collective-permute-start.25 = (f32[384,384]{1,0:T(8,128)}, f32[384,384]{1,0:T(8,128)}, u32[]{:S(2)}, u32[]{:S(2)}) collective-permute-start(f32[384,384]{1,0:T(8,128)} %copy.40), channel_id=1, source_target_pairs={{0,508},{1,509},{2,510},{3,511},{4,0},{5,1},{6,2},{7,3},{8,4},{9,5... | collective-permute-start | bytes 1769480 | tf_op jit(solution)/shard_map/ppermute | solution.py:11
  408.6 45.7 %collective-permute-start.22 = (f32[384,384]{1,0:T(8,128)}, f32[384,384]{1,0:T(8,128)}, u32[]{:S(2)}, u32[]{:S(2)}) collective-permute-start(f32[384,384]{1,0:T(8,128)} %copy.40), channel_id=1, source_target_pairs={{0,4},{1,5},{2,6},{3,7},{4,8},{5,9},{6,10},{7,11},{8,12},{9,13},{1... | collective-permute-start | bytes 1769480 | tf_op jit(solution)/shard_map/ppermute | solution.py:11
  410.5 56.3 %collective-permute-start.23 = (f32[384,384]{0,1:T(8,128)}, f32[384,384]{0,1:T(8,128)}, u32[]{:S(2)}, u32[]{:S(2)}) collective-permute-start(f32[384,384]{0,1:T(8,128)} %get-tuple-element.554), channel_id=1, source_target_pairs={{0,4},{1,5},{2,6},{3,7},{4,8},{5,9},{6,10},{7,11},{8,12},{9,13},{1... | collective-permute-start | bytes 1769480 | tf_op jit(solution)/shard_map/ppermute | solution.py:11
  412.4 54.4 %collective-permute-start.24 = (f32[384,384]{1,0:T(8,128)}, f32[384,384]{1,0:T(8,128)}, u32[]{:S(2)}, u32[]{:S(2)}) collective-permute-start(f32[384,384]{1,0:T(8,128)} %get-tuple-element.555), channel_id=1, source_target_pairs={{0,508},{1,509},{2,510},{3,511},{4,0},{5,1},{6,2},{7,3},{8,4},{9,5... | collective-permute-start | bytes 1769480 | tf_op jit(solution)/shard_map/ppermute | solution.py:11
  477.5 21.9 %collective-permute-start.28 = (f32[384,384]{1,0:T(8,128)}, f32[384,384]{1,0:T(8,128)}, u32[]{:S(2)}, u32[]{:S(2)}) collective-permute-start(f32[384,384]{1,0:T(8,128)} %get-tuple-element.558), channel_id=1, source_target_pairs={{0,510},{1,511},{2,0},{3,1},{4,2},{5,3},{6,4},{7,5},{8,6},{9,7},{1... | collective-permute-start | bytes 1769480 | tf_op jit(solution)/shard_map/ppermute | solution.py:11
  502.4 41.8 %collective-permute-start.33 = (f32[384,384]{1,0:T(8,128)}, f32[384,384]{1,0:T(8,128)}, u32[]{:S(2)}, u32[]{:S(2)}) collective-permute-start(f32[384,384]{1,0:T(8,128)} %copy.46), channel_id=1, source_target_pairs={{0,511},{1,0},{2,1},{3,2},{4,3},{5,4},{6,5},{7,6},{8,7},{9,8},{10,... | collective-permute-start | bytes 1769480 | tf_op jit(solution)/shard_map/ppermute | solution.py:11
  (15 other events, 204.3 us)
where the time goes:
time: 578 us; the launch traced here: 574 us
  waiting for transfers between devices  309 us (53%)
  starting transfers between devices  216 us (37%)
  local copies, waits for them, and re-layouts  24 us (4%)
  matrix products  16.6 us (3%)
    ppermute x34, waiting for transfers between devices, passed_along(): lax.ppermute(array, axis, [(i, (i + by) % peers) for i in range(peers)])  309 us
    ppermute x34, starting transfers between devices, passed_along(): lax.ppermute(array, axis, [(i, (i + by) % peers) for i in range(peers)])  216 us
    dot_general x8, matrix products, product(): jnp.dot(left, right, precision=lax.Precision.HIGHEST, preferred_element_t...  16.6 us
    broadcast_in_dim x17, local copies, waits for them, and re-layouts, body(): zeros = jnp.zeros((width, width), jnp.float32)  13 us
  transfers between devices with their start and end apart: 34, of which 25 were waited for; matrix products, arithmetic and copies ran while one was open for 1% of the time, Pallas kernels for 0%

commit v1 on v0

v1 whole, which is shorter than its diff:
```python
import functools

import jax
import jax.numpy as jnp
from jax import lax
from jax.experimental import pallas as pl
from jax.experimental.pallas import tpu as pltpu
from jax.sharding import PartitionSpec as P

MESH = pl.DeviceIdType.MESH
F32 = jnp.float32
BF16 = jnp.bfloat16
row_offset = 3
PIECES = 3


def split(value):
    high = value.astype(BF16)
    return high, (value - high.astype(F32)).astype(BF16)


def mm(a, b):
    return jnp.dot(a, b, preferred_element_type=F32)


def kernel(
    n,
    inv_ref, low_ref, up_ref,
    diag_ref, cross_ref,
    sig, wf, af, dpk, a_hi, a_lo, at_hi, at_lo, s_hi, s_lo,
    send_sem, recv_sem, pk_send, pk_recv,
):
    B = inv_ref.shape[1]
    Q = B // PIECES
    place = lax.axis_index("tm")
    t = (place + row_offset) % n
    s = jnp.int32(1)
    even = jnp.bool_(True) if (n.bit_length() - 2) % 2 == 0 else jnp.bool_(False)
    for k in range(1, n.bit_length() - 1):
        divides = t % (2**k) == 0
        s = jnp.where(divides, 2**k, s)
        even = jnp.where(divides, (n.bit_length() - 2 - k) % 2 == 0, even)
    is_zero = t == 0
    is_top = t == n // 2
    normal = jnp.logical_not(is_zero)
    has_children = jnp.logical_and(normal, s > 1)
    odd = jnp.logical_and(normal, jnp.logical_not(even))
    second = jnp.logical_and(jnp.logical_and(normal, even), jnp.logical_not(is_top))
    is_left = jnp.logical_and(t % (4 * s) == s, jnp.logical_not(is_top))
    parent = jnp.where(is_left, t + s, t - s)
    parent_left = parent % (8 * s) == 2 * s
    side = jnp.where(is_left == parent_left, 0, 1)
    half = s // 2
    g_half = jnp.where(is_left, 0, 1)

    def device(pos):
        return ((pos + (n - row_offset)) % n,)

    parent_dev = device(parent)
    child_dev = (
        device(t + jnp.where(is_left, -half, half)),
        device(t + jnp.where(is_left, half, -half)),
    )
    top_dev = (jnp.int32((n // 2 - row_offset) % n),)

    barrier = pltpu.get_barrier_semaphore()

    @pl.when(normal)
    def _():
        pl.semaphore_signal(barrier, inc=1, device_id=parent_dev, device_id_type=MESH)

    @pl.when(has_children)
    def _():
        for child in child_dev:
            pl.semaphore_signal(barrier, inc=1, device_id=child, device_id_type=MESH)

    @pl.when(is_zero)
    def _():
        pl.semaphore_signal(barrier, inc=1, device_id=top_dev, device_id_type=MESH)

    @pl.when(has_children)
    def _():
        pl.semaphore_wait(barrier, 3)

    @pl.when(jnp.logical_not(has_children))
    def _():
        pl.semaphore_wait(barrier, 1)

    def tri(i):
        return pl.ds(i * Q, Q), pl.ds(i * Q, B - i * Q)

    def to_child(c, k, src, dst, dev=None):
        return pltpu.make_async_remote_copy(
            src_ref=src, dst_ref=dst, send_sem=send_sem.at[c, k], recv_sem=recv_sem.at[k],
            device_id=child_dev[c] if dev is None else dev, device_id_type=MESH)

    def send_other(c, slot):
        for i in range(PIECES):
            to_child(c, i, sig.at[(slot, *tri(i))], sig.at[(0, *tri(i))]).start()

    def send_cross(c):
        for i in range(PIECES):
            rows = pl.ds(i * Q, Q)
            to_child(c, 3 + i, wf.at[c, rows], sig.at[1, rows]).start()

    def send_newest(c):
        for i in range(PIECES):
            to_child(c, 6 + i, sig.at[(4, *tri(i))], sig.at[(2, *tri(i))]).start()

    def recv(k):
        i = k % 3
        if k // 3 == 1:
            ref = sig.at[1, pl.ds(i * Q, Q)]
        else:
            ref = sig.at[(k // 3, *tri(i))]
        return ref, to_child(0, k, ref, ref)

    def packet(c):
        copies = []
        for i in range(2):
            copies.append((af.at[1, i], af.at[0, i]))
        for i in range(PIECES):
            copies.append((inv_ref.at[(0, *tri(i))], dpk.at[(0, *tri(i))]))
        return [
            pltpu.make_async_remote_copy(
                src_ref=src, dst_ref=dst, send_sem=pk_send.at[c, k], recv_sem=pk_recv.at[k],
                device_id=child_dev[c], device_id_type=MESH)
            for k, (src, dst) in enumerate(copies)
        ]

    def mirror(ref, slot):
        for i in range(PIECES):
            for j in range(i + 1, PIECES):
                ref[slot, j * Q:(j + 1) * Q, i * Q:(i + 1) * Q] = ref[slot, i * Q:(i + 1) * Q, j * Q:(j + 1) * Q].T

    zero_sends = [
        to_child(0, 6 + i, inv_ref.at[(0, *tri(i))], sig.at[(2, *tri(i))], dev=top_dev) for i in range(PIECES)
    ]

    @pl.when(is_zero)
    def _():
        for copy in zero_sends:
            copy.start()
        diag_ref[...] = inv_ref[...]
        cross_ref[...] = jnp.zeros_like(cross_ref)
        for copy in zero_sends:
            copy.wait_send()

    @pl.when(odd & has_children)
    def _():
        for c in range(2):
            for copy in packet(c)[2:]:
                copy.start()

    def prepare(i):
        for h in range(2):
            hi, lo = split(af[i, h])
            cols = slice(h * B, (h + 1) * B)
            a_hi[i, :, cols] = hi
            a_lo[i, :, cols] = lo
            hi_t, lo_t = split(af[i, h].T)
            at_hi[i, cols, :] = hi_t
            at_lo[i, cols, :] = lo_t

    def put_s(row, col, value):
        hi, lo = split(value)
        rows, cols = slice(row * B, (row + 1) * B), slice(col * B, (col + 1) * B)
        s_hi[rows, cols] = hi
        s_lo[rows, cols] = lo

    @pl.when(normal)
    def _():
        dpk[1] = inv_ref[0]
        d_hi, d_lo = split(inv_ref[0])
        for ref, where in ((low_ref, g_half), (up_ref, 1 - g_half)):
            hi, lo = split(ref[0])
            af[1, where] = mm(d_hi, hi) + mm(d_hi, lo) + mm(d_lo, hi)

        @pl.when(odd & has_children)
        def _():
            for c in range(2):
                for copy in packet(c)[:2]:
                    copy.start()

        prepare(1)

        @pl.when(second)
        def _():
            for copy in packet(0):
                copy.wait_recv()
            mirror(dpk, 0)
            prepare(0)

        @pl.when(is_top)
        def _():
            sig[0] = jnp.zeros((B, B), F32)
            sig[1] = jnp.zeros((B, B), F32)
            for k in range(6, 9):
                recv(k)[1].wait_recv()

        @pl.when(jnp.logical_not(is_top))
        def _():
            for k in range(9):
                ref, copy = recv(k)
                copy.wait_recv()

                @pl.when(odd & has_children)
                def _():
                    for c in range(2):
                        to_child(c, k, ref, ref).start()

        sends = even & has_children
        other_x = jnp.where(is_top, 0, 2 * side)
        other_p = jnp.where(is_top, 2, 3)

        @pl.when(sends)
        def _():
            send_other(0, other_x)

        mirror(sig, 0)
        mirror(sig, 2)
        put_s(0, 0, sig[0])
        put_s(1, 0, sig[1])
        put_s(0, 1, sig[1].T)
        put_s(1, 1, sig[2])

        def stage(i, carry):
            own = i == 1
            w = -(mm(a_hi[i], s_hi[...]) + mm(a_hi[i], s_lo[...]) + mm(a_lo[i], s_hi[...]))
            wf[0] = w[:, :B]
            wf[1] = w[:, B:]

            @pl.when(own & sends)
            def _():
                send_other(1, other_p)
                send_cross(0)
                send_cross(1)

            w_hi, w_lo = split(w)
            new = dpk[i] - (mm(w_hi, at_hi[i]) + mm(w_hi, at_lo[i]) + mm(w_lo, at_hi[i]))
            sig[3 + i] = new

            @pl.when(own & sends)
            def _():
                send_newest(0)
                send_newest(1)

            @pl.when(jnp.logical_not(own))
            def _():
                span = pl.ds(pl.multiple_of(side * B, B), B)
                for ref in (s_hi, s_lo):
                    ref[0:B, 0:B] = ref[span, span]
                put_s(1, 0, wf[side])
                put_s(0, 1, wf[side].T)
                put_s(1, 1, new)

            return carry

        lax.fori_loop(jnp.where(second, 0, 1), 2, stage, jnp.int32(0))
        diag_ref[0] = sig[4]
        cross_ref[0] = wf[g_half]

        @pl.when(has_children)
        def _():
            for c in range(2):
                for k in range(9):
                    to_child(c, k, recv(k)[0], recv(k)[0]).wait_send()

        @pl.when(odd & has_children)
        def _():
            for c in range(2):
                for copy in packet(c):
                    copy.wait_send()


def body(inv_diag, low_coupling, up_coupling):
    n = lax.axis_size("tm")
    B = inv_diag.shape[1]
    vmem = pl.BlockSpec(memory_space=pltpu.VMEM)
    block = jax.ShapeDtypeStruct(inv_diag.shape, F32)
    return pl.pallas_call(
        functools.partial(kernel, n),
        out_shape=(block, block),
        in_specs=[vmem] * 3,
        out_specs=(vmem, vmem),
        scratch_shapes=[
            pltpu.VMEM((5, B, B), F32),
            pltpu.VMEM((2, B, B), F32),
            pltpu.VMEM((2, 2, B, B), F32),
            pltpu.VMEM((2, B, B), F32),
            pltpu.VMEM((2, B, 2 * B), BF16),
            pltpu.VMEM((2, B, 2 * B), BF16),
            pltpu.VMEM((2, 2 * B, B), BF16),
            pltpu.VMEM((2, 2 * B, B), BF16),
            pltpu.VMEM((2 * B, 2 * B), BF16),
            pltpu.VMEM((2 * B, 2 * B), BF16),
            pltpu.SemaphoreType.DMA((2, 9)),
            pltpu.SemaphoreType.DMA((9,)),
            pltpu.SemaphoreType.DMA((2, 5)),
            pltpu.SemaphoreType.DMA((5,)),
        ],
        compiler_params=pltpu.CompilerParams(
            collective_id=0, has_side_effects=True, vmem_limit_bytes=60 * 1024 * 1024
        ),
    )(inv_diag, low_coupling, up_coupling)


def solution(mesh):
    placed = (P("tm", None, None),) * 3
    return jax.shard_map(
        body,
        mesh=mesh,
        in_specs=placed,
        out_specs=(P("tm", None, None), P("tm", None, None)),
        check_vma=False,
    )
```

time: 578 us -> 191 us (0.33)
  the two profiles are of different devices: /device:TPU:4 before, /device:TPU:98 now
where the time goes in v1:
time: 191 us
  Pallas kernels  187 us (98%)
  local copies, waits for them, and re-layouts  2.8 us (1%)
    pallas_call x1, Pallas kernels, body(): pl.pallas_call(functools.partial(kernel, n), out_shape=(block, block), in...  187 us

profile of v1, /device:TPU:98, one launch (start us, length us, event | category | flops | bytes accessed | tf_op | source)
XLA Modules:
  0.0 190.6 jit_solution(15481728534968766342)
XLA Ops:
  0.6 187.1 %shard_map.50 = (f32[1,384,384]{2,1,0:T(8,128)}, f32[1,384,384]{2,1,0:T(8,128)}) custom-call(f32[1,384,384]{2,1,0:T(8,128)} %inv_ref.1, f32[1,384,384]{2,1,0:T(8,128)} %low_ref.1, f32[1,384,384]{2,1,0:T(8,128)} %up_ref.1), custom_call_target="tpu_custom_call" | custom-call | tf_op jit(solution)/shard_map/pallas_call | solution.py:281
  187.8 0.0 copy-start
  187.8 2.0 %copy.7 = f32[1,384,384]{2,1,0:T(8,128)} copy(f32[1,384,384]{2,1,0:T(8,128)} %get-tuple-element.4) | data formatting | bytes 1179648
  189.7 0.0 copy-done
  189.7 0.8 copy.8
Async XLA Ops:
  187.8 2.0 %copy-start = (f32[1,384,384]{2,1,0:T(8,128)S(1)}, f32[1,384,384]{2,1,0:T(8,128)}, u32[]{:S(2)}) copy-start(f32[1,384,384]{2,1,0:T(8,128)} %get-tuple-element.5) | copy-start | bytes 1769476

commit v2 on v1

v2 whole, which is shorter than its diff:
```python
import functools

import jax
import jax.numpy as jnp
from jax import lax
from jax.experimental import pallas as pl
from jax.experimental.pallas import tpu as pltpu
from jax.sharding import PartitionSpec as P

MESH = pl.DeviceIdType.MESH
F32 = jnp.float32
BF16 = jnp.bfloat16
row_offset = 3
PIECES = 6


def split(value):
    high = value.astype(BF16)
    return high, (value - high.astype(F32)).astype(BF16)


def mm(a, b):
    return jnp.dot(a, b, preferred_element_type=F32)


def kernel(
    n,
    inv_ref, low_ref, up_ref,
    diag_ref, cross_ref,
    sig, wf, af, dpk, a_hi, a_lo, at_hi, at_lo, s_hi, s_lo,
    send_sem, recv_sem, pk_send, pk_recv,
):
    B = inv_ref.shape[1]
    Q = B // 3
    H = B // PIECES
    place = lax.axis_index("tm")
    t = (place + row_offset) % n
    s = jnp.int32(1)
    top_level = n.bit_length() - 2
    even = jnp.bool_(top_level % 2 == 0)
    for k in range(1, n.bit_length() - 1):
        divides = t % (2**k) == 0
        s = jnp.where(divides, 2**k, s)
        even = jnp.where(divides, (top_level - k) % 2 == 0, even)
    is_zero = t == 0
    is_top = t == n // 2
    normal = jnp.logical_not(is_zero)
    odd = jnp.logical_and(normal, jnp.logical_not(even))
    second = jnp.logical_and(jnp.logical_and(normal, even), jnp.logical_not(is_top))
    is_left = jnp.logical_and(t % (4 * s) == s, jnp.logical_not(is_top))
    parent = jnp.where(is_left, t + s, t - s)
    parent_left = parent % (8 * s) == 2 * s
    side = jnp.where(is_left == parent_left, 0, 1)
    half = s // 2
    g_half = jnp.where(is_left, 0, 1)
    to_x = jnp.where(is_left, -1, 1)

    first_round = jnp.logical_and(normal, s >= n // 8)
    source = jnp.logical_and(normal & even, s > 1)
    lower = jnp.logical_and(second & first_round, is_left)
    upper = jnp.logical_and(second & first_round, jnp.logical_not(is_left))
    late_second = jnp.logical_and(second, jnp.logical_not(first_round))
    late_odd = jnp.logical_and(odd, jnp.logical_not(first_round))
    near = jnp.logical_and(late_second, side == 1)
    has_next = odd | lower | near
    reach = jnp.where(is_top, half, half // 2)
    first_x = t + to_x * reach
    first_p = t - to_x * reach
    after = jnp.where(odd & first_round, t - half, jnp.where(lower, t + 2 * s, jnp.where(near, parent, t + to_x * half)))
    before = jnp.where(
        is_top, 0,
        jnp.where(odd & first_round, n // 2, jnp.where(
            upper, t - 2 * s, jnp.where(near, 2 * t - parent, jnp.where(late_odd, t - to_x * half, parent)))))
    near_child = t - to_x * half

    def device(pos):
        return ((pos + (n - row_offset)) % n,)

    ends = (device(first_x), device(first_p), device(after))
    top_dev, quarter_dev, zero_dev = device(jnp.int32(n // 2)), device(jnp.int32(n // 4)), device(jnp.int32(0))
    at_quarter = t == n // 4

    barrier = pltpu.get_barrier_semaphore()

    def greet(dev):
        pl.semaphore_signal(barrier, inc=1, device_id=dev, device_id_type=MESH)

    @pl.when(normal)
    def _():
        greet(device(before))

    @pl.when(near)
    def _():
        greet(device(parent))

    @pl.when(at_quarter)
    def _():
        greet(zero_dev)

    def number(flag):
        return jnp.where(flag, 1, 0)

    peers = 2 * number(is_zero) + 2 * number(source) + number(has_next) + number(late_odd)

    @pl.when(peers > 0)
    def _():
        pl.semaphore_wait(barrier, peers)

    def tri(i):
        start = i * H // Q * Q
        return pl.ds(i * H, H), pl.ds(start, B - start)

    def piece(slot, i, whole):
        return sig.at[slot, pl.ds(i * H, H)] if whole else sig.at[(slot, *tri(i))]

    def copy_to(e, k, src, dst, dev=None):
        return pltpu.make_async_remote_copy(
            src_ref=src, dst_ref=dst, send_sem=send_sem.at[e, k], recv_sem=recv_sem.at[k],
            device_id=ends[e] if dev is None else dev, device_id_type=MESH)

    def target(k):
        return piece(k // PIECES, k % PIECES, k // PIECES == 1)

    def send(e, part, source_of):
        for i in range(PIECES):
            k = part * PIECES + i
            copy_to(e, k, source_of(i), target(k)).start()

    def send_other(e, slot):
        send(e, 0, lambda i: piece(slot, i, False))

    def send_cross(e):
        send(e, 1, lambda i: wf.at[e, pl.ds(i * H, H)])

    def send_newest(e):
        send(e, 2, lambda i: piece(4, i, False))

    KINDS = 3 * PIECES

    def packet_parts():
        parts = [(inv_ref.at[(0, *tri(i))], dpk.at[(0, *tri(i))]) for i in range(PIECES)]
        parts += [(af.at[1, i // 2, pl.ds(i % 2 * B // 2, B // 2)], af.at[0, i // 2, pl.ds(i % 2 * B // 2, B // 2)]) for i in range(4)]
        return parts

    PARTS = PIECES + 4

    def packet(e, k, src, dst, dev):
        return pltpu.make_async_remote_copy(
            src_ref=src, dst_ref=dst, send_sem=pk_send.at[e, k], recv_sem=pk_recv.at[k],
            device_id=dev, device_id_type=MESH)

    def send_packet(chosen):
        for k in chosen:
            src, dst = packet_parts()[k]
            packet(0, k, src, dst, ends[2]).start()

            @pl.when(late_odd)
            def _():
                packet(1, k, src, dst, device(near_child)).start()

    def mirror(ref, slot):
        for i in range(3):
            for j in range(i + 1, 3):
                ref[slot, j * Q:(j + 1) * Q, i * Q:(i + 1) * Q] = ref[slot, i * Q:(i + 1) * Q, j * Q:(j + 1) * Q].T

    def zero_sends():
        out = []
        for i in range(PIECES):
            src = inv_ref.at[(0, *tri(i))]
            out.append(copy_to(0, 2 * PIECES + i, src, target(2 * PIECES + i), top_dev))
        for i in range(PIECES):
            src = inv_ref.at[(0, *tri(i))]
            out.append(copy_to(1, i, src, target(i), quarter_dev))
        return out

    @pl.when(is_zero)
    def _():
        for copy in zero_sends():
            copy.start()
        diag_ref[...] = inv_ref[...]
        cross_ref[...] = jnp.zeros_like(cross_ref)
        for copy in zero_sends():
            copy.wait_send()

    @pl.when(odd)
    def _():
        send_packet(range(PIECES))

    @pl.when(is_top)
    def _():
        sig[0] = jnp.zeros((B, B), F32)
        sig[1] = jnp.zeros((B, B), F32)
        send_other(0, 0)
        send(0, 1, lambda i: piece(1, i, True))

    def prepare(i):
        for h in range(2):
            hi, lo = split(af[i, h])
            cols = slice(h * B, (h + 1) * B)
            a_hi[i, :, cols] = hi
            a_lo[i, :, cols] = lo
            hi_t, lo_t = split(af[i, h].T)
            at_hi[i, cols, :] = hi_t
            at_lo[i, cols, :] = lo_t

    def put_s(row, col, value):
        hi, lo = split(value)
        rows, cols = slice(row * B, (row + 1) * B), slice(col * B, (col + 1) * B)
        s_hi[rows, cols] = hi
        s_lo[rows, cols] = lo

    @pl.when(normal)
    def _():
        dpk[1] = inv_ref[0]
        d_hi, d_lo = split(inv_ref[0])
        for ref, where in ((low_ref, g_half), (up_ref, 1 - g_half)):
            hi, lo = split(ref[0])
            af[1, where] = mm(d_hi, hi) + mm(d_hi, lo) + mm(d_lo, hi)

        @pl.when(odd)
        def _():
            send_packet(range(PIECES, PARTS))

        prepare(1)

        @pl.when(second)
        def _():
            for k, (_, dst) in enumerate(packet_parts()):
                packet(0, k, dst, dst, ends[2]).wait_recv()

                @pl.when(lower)
                def _():
                    packet(0, k, dst, dst, ends[2]).start()

            mirror(dpk, 0)
            prepare(0)

        @pl.when(is_top)
        def _():
            for k in range(2 * PIECES, KINDS):
                copy_to(2, k, target(k), target(k)).wait_recv()

        @pl.when(jnp.logical_not(is_top))
        def _():
            for k in range(KINDS):
                copy_to(2, k, target(k), target(k)).wait_recv()

                @pl.when(has_next)
                def _():
                    copy_to(2, k, target(k), target(k)).start()

        sends = source

        @pl.when(sends & jnp.logical_not(is_top))
        def _():
            send_other(0, 2 * side)

        mirror(sig, 0)
        mirror(sig, 2)
        put_s(0, 0, sig[0])
        put_s(1, 0, sig[1])
        put_s(0, 1, sig[1].T)
        put_s(1, 1, sig[2])

        def stage(i, carry):
            own = i == 1
            w = -(mm(a_hi[i], s_hi[...]) + mm(a_hi[i], s_lo[...]) + mm(a_lo[i], s_hi[...]))
            wf[0] = w[:, :B]
            wf[1] = w[:, B:]

            @pl.when(own & sends)
            def _():
                @pl.when(jnp.logical_not(is_top))
                def _():
                    send_other(1, 3)
                    send_cross(0)

                send_cross(1)

            w_hi, w_lo = split(w)
            new = dpk[i] - (mm(w_hi, at_hi[i]) + mm(w_hi, at_lo[i]) + mm(w_lo, at_hi[i]))
            sig[3 + i] = new

            @pl.when(own & sends)
            def _():
                send_newest(0)
                send_newest(1)

            @pl.when(jnp.logical_not(own))
            def _():
                span = pl.ds(pl.multiple_of(side * B, B), B)
                for ref in (s_hi, s_lo):
                    ref[0:B, 0:B] = ref[span, span]
                put_s(1, 0, wf[side])
                put_s(0, 1, wf[side].T)
                put_s(1, 1, new)

            return carry

        lax.fori_loop(jnp.where(second, 0, 1), 2, stage, jnp.int32(0))
        diag_ref[0] = sig[4]
        cross_ref[0] = wf[g_half]

        def drain(e, kinds):
            for k in kinds:
                copy_to(e, k, target(k), target(k)).wait_send()

        @pl.when(source)
        def _():
            drain(0, range(KINDS))
            drain(1, range(PIECES, KINDS))

        @pl.when(source & jnp.logical_not(is_top))
        def _():
            drain(1, range(PIECES))

        @pl.when(has_next)
        def _():
            drain(2, range(KINDS))

        def drain_packet(e):
            for k, (src, dst) in enumerate(packet_parts()):
                packet(e, k, src, dst, ends[2]).wait_send()

        @pl.when(odd | lower)
        def _():
            drain_packet(0)

        @pl.when(late_odd)
        def _():
            drain_packet(1)


def body(inv_diag, low_coupling, up_coupling):
    n = lax.axis_size("tm")
    B = inv_diag.shape[1]
    vmem = pl.BlockSpec(memory_space=pltpu.VMEM)
    block = jax.ShapeDtypeStruct(inv_diag.shape, F32)
    return pl.pallas_call(
        functools.partial(kernel, n),
        out_shape=(block, block),
        in_specs=[vmem] * 3,
        out_specs=(vmem, vmem),
        scratch_shapes=[
            pltpu.VMEM((5, B, B), F32),
            pltpu.VMEM((2, B, B), F32),
            pltpu.VMEM((2, 2, B, B), F32),
            pltpu.VMEM((2, B, B), F32),
            pltpu.VMEM((2, B, 2 * B), BF16),
            pltpu.VMEM((2, B, 2 * B), BF16),
            pltpu.VMEM((2, 2 * B, B), BF16),
            pltpu.VMEM((2, 2 * B, B), BF16),
            pltpu.VMEM((2 * B, 2 * B), BF16),
            pltpu.VMEM((2 * B, 2 * B), BF16),
            pltpu.SemaphoreType.DMA((3, 3 * PIECES)),
            pltpu.SemaphoreType.DMA((3 * PIECES,)),
            pltpu.SemaphoreType.DMA((2, PIECES + 4)),
            pltpu.SemaphoreType.DMA((PIECES + 4,)),
        ],
        compiler_params=pltpu.CompilerParams(
            collective_id=0, has_side_effects=True, vmem_limit_bytes=60 * 1024 * 1024
        ),
    )(inv_diag, low_coupling, up_coupling)


def solution(mesh):
    placed = (P("tm", None, None),) * 3
    return jax.shard_map(
        body,
        mesh=mesh,
        in_specs=placed,
        out_specs=(P("tm", None, None), P("tm", None, None)),
        check_vma=False,
    )
```

time: 191 us -> 154 us (0.81)
  the two profiles are of different devices: /device:TPU:98 before, /device:TPU:94 now
where the time goes in v2:
time: 154 us
  Pallas kernels  150 us (97%)
  local copies, waits for them, and re-layouts  2.8 us (2%)
    pallas_call x1, Pallas kernels, body(): pl.pallas_call(functools.partial(kernel, n), out_shape=(block, block), in...  150 us

profile of v2, /device:TPU:94, one launch (start us, length us, event | category | flops | bytes accessed | tf_op | source)
XLA Modules:
  0.0 153.5 jit_solution(2500802901978667237)
XLA Ops:
  0.6 150.1 %shard_map.50 = (f32[1,384,384]{2,1,0:T(8,128)}, f32[1,384,384]{2,1,0:T(8,128)}) custom-call(f32[1,384,384]{2,1,0:T(8,128)} %inv_ref.1, f32[1,384,384]{2,1,0:T(8,128)} %low_ref.1, f32[1,384,384]{2,1,0:T(8,128)} %up_ref.1), custom_call_target="tpu_custom_call" | custom-call | tf_op jit(solution)/shard_map/pallas_call | solution.py:339
  150.7 0.0 copy-start
  150.7 2.0 %copy.7 = f32[1,384,384]{2,1,0:T(8,128)} copy(f32[1,384,384]{2,1,0:T(8,128)} %get-tuple-element.4) | data formatting | bytes 1179648
  152.7 0.0 copy-done
  152.7 0.8 copy.8
Async XLA Ops:
  150.7 2.0 %copy-start = (f32[1,384,384]{2,1,0:T(8,128)S(1)}, f32[1,384,384]{2,1,0:T(8,128)}, u32[]{:S(2)}) copy-start(f32[1,384,384]{2,1,0:T(8,128)} %get-tuple-element.5) | copy-start | bytes 1769476

commit v3 on v2

--- a/solution.py
+++ b/solution.py
@@ -28,7 +28,7 @@
     inv_ref, low_ref, up_ref,
     diag_ref, cross_ref,
     sig, wf, af, dpk, a_hi, a_lo, at_hi, at_lo, s_hi, s_lo,
-    send_sem, recv_sem, pk_send, pk_recv,
+    send_sem, recv_sem, pk_send, pk_recv, go_sem,
 ):
     B = inv_ref.shape[1]
     Q = B // 3
@@ -57,28 +57,31 @@
 
     first_round = jnp.logical_and(normal, s >= n // 8)
     source = jnp.logical_and(normal & even, s > 1)
+    right = first_round & (t > n // 2)
     lower = jnp.logical_and(second & first_round, is_left)
-    upper = jnp.logical_and(second & first_round, jnp.logical_not(is_left))
-    late_second = jnp.logical_and(second, jnp.logical_not(first_round))
     late_odd = jnp.logical_and(odd, jnp.logical_not(first_round))
-    near = jnp.logical_and(late_second, side == 1)
-    has_next = odd | lower | near
-    reach = jnp.where(is_top, half, half // 2)
-    first_x = t + to_x * reach
-    first_p = t - to_x * reach
-    after = jnp.where(odd & first_round, t - half, jnp.where(lower, t + 2 * s, jnp.where(near, parent, t + to_x * half)))
+    near = jnp.logical_and(second, side == 1)
+    has_next = (second & jnp.logical_not(right)) | (right & (t < 7 * n // 8))
+    first_x = t + to_x * jnp.where(is_top, half, half // 2)
+    first_p = t - to_x * (half // 2)
+    after = jnp.where(right, jnp.where(odd, t - half, t + n // 4), jnp.where(near, 2 * parent - t, parent))
     before = jnp.where(
         is_top, 0,
-        jnp.where(odd & first_round, n // 2, jnp.where(
-            upper, t - 2 * s, jnp.where(near, 2 * t - parent, jnp.where(late_odd, t - to_x * half, parent)))))
+        jnp.where(right, jnp.where(odd, n // 2, jnp.where(lower, parent, t - n // 4)), jnp.where(
+            near, 2 * t - parent, jnp.where(odd, t + to_x * half, 2 * parent - t))))
+    packet_from = jnp.where(first_round & jnp.logical_not(lower), t - n // 4, parent)
+    packet_to = jnp.where(odd & first_round, t - half, jnp.where(lower, t + n // 4, t + to_x * half))
     near_child = t - to_x * half
+    held = normal & is_left & (s == n // 16)
+    holder = normal & (s == n // 8)
 
     def device(pos):
         return ((pos + (n - row_offset)) % n,)
 
     ends = (device(first_x), device(first_p), device(after))
-    top_dev, quarter_dev, zero_dev = device(jnp.int32(n // 2)), device(jnp.int32(n // 4)), device(jnp.int32(0))
-    at_quarter = t == n // 4
+    top_dev, start_dev, zero_dev = device(jnp.int32(n // 2)), device(jnp.int32(3 * n // 8)), device(jnp.int32(0))
+    at_start = t == 3 * n // 8
+    held_dev = device(t - n // 16)
 
     barrier = pltpu.get_barrier_semaphore()
 
@@ -89,18 +92,24 @@
     def _():
         greet(device(before))
 
-    @pl.when(near)
+    @pl.when(second)
+    def _():
+        greet(device(packet_from))
+
+    @pl.when(at_start)
+    def _():
+        greet(zero_dev)
+
+    @pl.when(held)
     def _():
         greet(device(parent))
-
-    @pl.when(at_quarter)
-    def _():
-        greet(zero_dev)
 
     def number(flag):
         return jnp.where(flag, 1, 0)
 
-    peers = 2 * number(is_zero) + 2 * number(source) + number(has_next) + number(late_odd)
+    peers = (
+        2 * number(is_zero) + 2 * number(source) + number(has_next) + 2 * number(late_odd)
+        + number(odd & first_round) + number(lower) + (number(holder) if n >= 32 else 0))
 
     @pl.when(peers > 0)
     def _():
@@ -149,14 +158,10 @@
             src_ref=src, dst_ref=dst, send_sem=pk_send.at[e, k], recv_sem=pk_recv.at[k],
             device_id=dev, device_id_type=MESH)
 
-    def send_packet(chosen):
+    def send_packet(e, chosen, dev):
         for k in chosen:
             src, dst = packet_parts()[k]
-            packet(0, k, src, dst, ends[2]).start()
-
-            @pl.when(late_odd)
-            def _():
-                packet(1, k, src, dst, device(near_child)).start()
+            packet(e, k, src, dst, dev).start()
 
     def mirror(ref, slot):
         for i in range(3):
@@ -170,7 +175,7 @@
             out.append(copy_to(0, 2 * PIECES + i, src, target(2 * PIECES + i), top_dev))
         for i in range(PIECES):
             src = inv_ref.at[(0, *tri(i))]
-            out.append(copy_to(1, i, src, target(i), quarter_dev))
+            out.append(copy_to(1, i, src, target(i), start_dev))
         return out
 
     @pl.when(is_zero)
@@ -182,16 +187,20 @@
         for copy in zero_sends():
             copy.wait_send()
 
+    early = late_odd & jnp.logical_not(held)
+
     @pl.when(odd)
     def _():
-        send_packet(range(PIECES))
-
-    @pl.when(is_top)
+        send_packet(0, range(PIECES), device(packet_to))
+
+    @pl.when(early)
+    def _():
+        send_packet(1, range(PIECES), device(near_child))
+
+    @pl.when(is_top | right)
     def _():
         sig[0] = jnp.zeros((B, B), F32)
         sig[1] = jnp.zeros((B, B), F32)
-        send_other(0, 0)
-        send(0, 1, lambda i: piece(1, i, True))
 
     def prepare(i):
         for h in range(2):
@@ -219,35 +228,50 @@
 
         @pl.when(odd)
         def _():
-            send_packet(range(PIECES, PARTS))
+            send_packet(0, range(PIECES, PARTS), device(packet_to))
+
+        @pl.when(early)
+        def _():
+            send_packet(1, range(PIECES, PARTS), device(near_child))
 
         prepare(1)
 
+        if n >= 32:
+            @pl.when(held)
+            def _():
+                pl.semaphore_wait(go_sem, 1)
+                send_packet(1, range(PARTS), device(near_child))
+
         @pl.when(second)
         def _():
             for k, (_, dst) in enumerate(packet_parts()):
-                packet(0, k, dst, dst, ends[2]).wait_recv()
+                packet(0, k, dst, dst, zero_dev).wait_recv()
 
                 @pl.when(lower)
                 def _():
-                    packet(0, k, dst, dst, ends[2]).start()
+                    packet(0, k, dst, dst, device(packet_to)).start()
 
             mirror(dpk, 0)
             prepare(0)
 
-        @pl.when(is_top)
-        def _():
-            for k in range(2 * PIECES, KINDS):
-                copy_to(2, k, target(k), target(k)).wait_recv()
-
-        @pl.when(jnp.logical_not(is_top))
-        def _():
-            for k in range(KINDS):
+        def receive(kinds):
+            for k in kinds:
                 copy_to(2, k, target(k), target(k)).wait_recv()
 
                 @pl.when(has_next)
                 def _():
                     copy_to(2, k, target(k), target(k)).start()
+
+        @pl.when(jnp.logical_not(is_top | right))
+        def _():
+            receive(range(2 * PIECES))
+
+        receive(range(2 * PIECES, KINDS))
+
+        if n >= 32:
+            @pl.when(holder)
+            def _():
+                pl.semaphore_signal(go_sem, inc=1, device_id=held_dev, device_id_type=MESH)
 
         sends = source
 
@@ -272,7 +296,6 @@
             def _():
                 @pl.when(jnp.logical_not(is_top))
                 def _():
-                    send_other(1, 3)
                     send_cross(0)
 
                 send_cross(1)
@@ -285,6 +308,10 @@
             def _():
                 send_newest(0)
                 send_newest(1)
+
+            @pl.when(jnp.logical_not(own) & sends)
+            def _():
+                send_other(1, 3)
 
             @pl.when(jnp.logical_not(own))
             def _():
@@ -307,20 +334,25 @@
 
         @pl.when(source)
         def _():
-            drain(0, range(KINDS))
+            drain(0, range(2 * PIECES, KINDS))
             drain(1, range(PIECES, KINDS))
 
         @pl.when(source & jnp.logical_not(is_top))
         def _():
+            drain(0, range(2 * PIECES))
             drain(1, range(PIECES))
 
         @pl.when(has_next)
         def _():
-            drain(2, range(KINDS))
+            drain(2, range(2 * PIECES, KINDS))
+
+        @pl.when(has_next & jnp.logical_not(right))
+        def _():
+            drain(2, range(2 * PIECES))
 
         def drain_packet(e):
             for k, (src, dst) in enumerate(packet_parts()):
-                packet(e, k, src, dst, ends[2]).wait_send()
+                packet(e, k, src, dst, zero_dev).wait_send()
 
         @pl.when(odd | lower)
         def _():
@@ -356,6 +388,7 @@
             pltpu.SemaphoreType.DMA((3 * PIECES,)),
             pltpu.SemaphoreType.DMA((2, PIECES + 4)),
             pltpu.SemaphoreType.DMA((PIECES + 4,)),
+            pltpu.SemaphoreType.REGULAR,
         ],
         compiler_params=pltpu.CompilerParams(
             collective_id=0, has_side_effects=True, vmem_limit_bytes=60 * 1024 * 1024

time: 154 us -> 169 us (1.097)
  the two profiles are of different devices: /device:TPU:94 before, /device:TPU:88 now
where the time goes in v3:
time: 169 us
  Pallas kernels  165 us (98%)
  local copies, waits for them, and re-layouts  2.8 us (2%)
    pallas_call x1, Pallas kernels, body(): pl.pallas_call(functools.partial(kernel, n), out_shape=(block, block), in...  165 us

profile of v3, /device:TPU:88, one launch (start us, length us, event | category | flops | bytes accessed | tf_op | source)
XLA Modules:
  0.0 168.8 jit_solution(2242635381589028810)
XLA Ops:
  0.6 165.4 %shard_map.50 = (f32[1,384,384]{2,1,0:T(8,128)}, f32[1,384,384]{2,1,0:T(8,128)}) custom-call(f32[1,384,384]{2,1,0:T(8,128)} %inv_ref.1, f32[1,384,384]{2,1,0:T(8,128)} %low_ref.1, f32[1,384,384]{2,1,0:T(8,128)} %up_ref.1), custom_call_target="tpu_custom_call" | custom-call | tf_op jit(solution)/shard_map/pallas_call | solution.py:371
  166.0 0.0 copy-start
  166.0 2.0 %copy.7 = f32[1,384,384]{2,1,0:T(8,128)} copy(f32[1,384,384]{2,1,0:T(8,128)} %get-tuple-element.4) | data formatting | bytes 1179648
  168.0 0.0 copy-done
  168.0 0.8 copy.8
Async XLA Ops:
  166.0 2.0 %copy-start = (f32[1,384,384]{2,1,0:T(8,128)S(1)}, f32[1,384,384]{2,1,0:T(8,128)}, u32[]{:S(2)}) copy-start(f32[1,384,384]{2,1,0:T(8,128)} %get-tuple-element.5) | copy-start | bytes 1769476

commit v4 on v3

v4 whole, which is shorter than its diff:
```python
import functools

import jax
import jax.numpy as jnp
from jax import lax
from jax.experimental import pallas as pl
from jax.experimental.pallas import tpu as pltpu
from jax.sharding import PartitionSpec as P

MESH = pl.DeviceIdType.MESH
F32 = jnp.float32
BF16 = jnp.bfloat16
row_offset = 3
PIECES = 6


def split(value):
    high = value.astype(BF16)
    return high, (value - high.astype(F32)).astype(BF16)


def mm(a, b):
    return jnp.dot(a, b, preferred_element_type=F32)


def kernel(
    n,
    inv_ref, low_ref, up_ref,
    diag_ref, cross_ref,
    sig, wf, tmp, af, dpk, a_hi, a_lo, at_hi, at_lo, s_hi, s_lo,
    send_sem, recv_sem, pk_send, pk_recv, res_send, res_recv, go_sem, call_sem,
):
    B = inv_ref.shape[1]
    Q = B // 3
    H = B // PIECES
    place = lax.axis_index("tm")
    t = (place + row_offset) % n
    s = jnp.int32(1)
    top_level = n.bit_length() - 2
    even = jnp.bool_(top_level % 2 == 0)
    for k in range(1, n.bit_length() - 1):
        divides = t % (2**k) == 0
        s = jnp.where(divides, 2**k, s)
        even = jnp.where(divides, (top_level - k) % 2 == 0, even)
    is_zero = t == 0
    is_top = t == n // 2
    normal = jnp.logical_not(is_zero)
    odd = jnp.logical_and(normal, jnp.logical_not(even))
    second = jnp.logical_and(jnp.logical_and(normal, even), jnp.logical_not(is_top))
    is_left = jnp.logical_and(t % (4 * s) == s, jnp.logical_not(is_top))
    parent = jnp.where(is_left, t + s, t - s)
    parent_left = parent % (8 * s) == 2 * s
    side = jnp.where(is_left == parent_left, 0, 1)
    half = s // 2
    g_half = jnp.where(is_left, 0, 1)
    to_x = jnp.where(is_left, -1, 1)

    first_round = jnp.logical_and(normal, s >= n // 8)
    source = jnp.logical_and(normal & even, s > 1)
    right = first_round & (t > n // 2)
    lower = jnp.logical_and(second & first_round, is_left)
    late_odd = jnp.logical_and(odd, jnp.logical_not(first_round))
    near = jnp.logical_and(second, side == 1)
    has_next = (near & jnp.logical_not(right)) | (right & (t < 7 * n // 8))
    first_x = t + to_x * jnp.where(is_top, half, half // 2)
    first_p = t - to_x * (half // 2)
    after = jnp.where(right, jnp.where(odd, t - half, t + n // 4), 2 * parent - t)
    before = jnp.where(
        is_top, 0,
        jnp.where(right, jnp.where(odd, n // 2, jnp.where(lower, parent, t - n // 4)), jnp.where(
            near, 2 * t - parent, 2 * parent - t)))
    packet_from = jnp.where(first_round & jnp.logical_not(lower), t - n // 4, parent)
    packet_to = jnp.where(odd & first_round, t - half, jnp.where(lower, t + n // 4, t + to_x * half))
    near_child = t - to_x * half
    feeds_cross = second & is_left
    feeds_sigma = second & (is_left == (s == 1))
    last_odd = odd & (s == 2)
    held = normal & is_left & (s == n // 16) & (t < 3 * n // 4)
    half_held = t == 5 * n // 16
    calls = held & jnp.logical_not(half_held)
    at_start = t == 3 * n // 8
    late_packet = (near & parent_left & (2 * s == n // 16) & (t < 3 * n // 4)) | at_start
    holder = lower | at_start

    bends = n >= 128
    hub = (t % 32 == 10) & bends
    bend_p = near & jnp.logical_not(is_left | first_round) & (s == 4) & bends
    bend_x = second & is_left & jnp.logical_not(near | first_round) & (s == 4) & bends
    bend_q = (s == 16) & normal & bends
    first_x = first_x - jnp.where(bend_q & is_left, 2, 0)
    first_p = first_p - jnp.where(bend_q & jnp.logical_not(is_left), 2, 0)
    before = jnp.where(hub, t + 6, jnp.where(bend_p, t - 2, jnp.where(bend_x, t + 6, before)))
    has_next = has_next & jnp.logical_not(bend_p)
    after = jnp.where(hub, t + 2, after)
    forwards = has_next & jnp.logical_not(late_packet)

    def device(pos):
        return ((pos + (n - row_offset)) % n,)

    ends = (device(first_x), device(first_p), device(after))
    top_dev, start_dev, zero_dev = device(jnp.int32(n // 2)), device(jnp.int32(3 * n // 8)), device(jnp.int32(0))
    held_dev = device(t - n // 16)

    barrier = pltpu.get_barrier_semaphore()

    def greet(dev):
        pl.semaphore_signal(barrier, inc=1, device_id=dev, device_id_type=MESH)

    @pl.when((normal & even) | right | hub)
    def _():
        greet(device(before))

    @pl.when(odd)
    def _():
        greet(device(t - half))

        @pl.when(jnp.logical_not(last_odd))
        def _():
            greet(device(t + half))

    if n >= 32:
        @pl.when(lower)
        def _():
            greet(held_dev)

    @pl.when(second)
    def _():
        greet(device(packet_from))

    @pl.when(at_start)
    def _():
        greet(zero_dev)

    @pl.when(held)
    def _():
        greet(device(parent))

    def number(flag):
        return jnp.where(flag, 1, 0)

    peers = (
        2 * number(is_zero) + 2 * number(source) + number(has_next) + 2 * number(late_odd)
        + number(odd & first_round) + number(lower) + number(feeds_cross) + number(feeds_sigma & (s > 1)) + (number(holder) + number(calls) if n >= 32 else 0) + 2 * number(hub))

    @pl.when(peers > 0)
    def _():
        pl.semaphore_wait(barrier, peers)

    def tri(i):
        start = i * H // Q * Q
        return pl.ds(i * H, H), pl.ds(start, B - start)

    def piece(slot, i, whole):
        return sig.at[slot, pl.ds(i * H, H)] if whole else sig.at[(slot, *tri(i))]

    def copy_to(e, k, src, dst, dev=None):
        return pltpu.make_async_remote_copy(
            src_ref=src, dst_ref=dst, send_sem=send_sem.at[e, k], recv_sem=recv_sem.at[k],
            device_id=ends[e] if dev is None else dev, device_id_type=MESH)

    def target(k):
        return piece(k // PIECES, k % PIECES, k // PIECES == 1)

    def send(e, part, source_of):
        for i in range(PIECES):
            k = part * PIECES + i
            copy_to(e, k, source_of(i), target(k)).start()

    def send_other(e, slot):
        send(e, 0, lambda i: piece(slot, i, False))

    def send_cross(e):
        send(e, 1, lambda i: wf.at[1, e, pl.ds(i * H, H)])

    def send_newest(e):
        send(e, 2, lambda i: piece(4, i, False))

    KINDS = 3 * PIECES

    def packet_parts():
        parts = [(inv_ref.at[(0, *tri(i))], dpk.at[(0, *tri(i))]) for i in range(PIECES)]
        parts += [(af.at[1, i // 3, pl.ds(i % 3 * Q, Q)], af.at[0, i // 3, pl.ds(i % 3 * Q, Q)]) for i in range(6)]
        return parts

    PARTS = PIECES + 6

    def packet(e, k, src, dst, dev):
        return pltpu.make_async_remote_copy(
            src_ref=src, dst_ref=dst, send_sem=pk_send.at[e, k], recv_sem=pk_recv.at[k],
            device_id=dev, device_id_type=MESH)

    def send_packet(e, chosen, dev):
        for k in chosen:
            src, dst = packet_parts()[k]
            packet(e, k, src, dst, dev).start()

    def mirror(ref, slot):
        for i in range(3):
            for j in range(i + 1, 3):
                ref[slot, j * Q:(j + 1) * Q, i * Q:(i + 1) * Q] = ref[slot, i * Q:(i + 1) * Q, j * Q:(j + 1) * Q].T

    def zero_sends():
        out = []
        for i in range(PIECES):
            src = inv_ref.at[(0, *tri(i))]
            out.append(copy_to(0, 2 * PIECES + i, src, target(2 * PIECES + i), top_dev))
        for i in range(PIECES):
            src = inv_ref.at[(0, *tri(i))]
            out.append(copy_to(1, i, src, target(i), start_dev))
        return out

    @pl.when(is_zero)
    def _():
        for copy in zero_sends():
            copy.start()
        diag_ref[...] = inv_ref[...]
        cross_ref[...] = jnp.zeros_like(cross_ref)
        for copy in zero_sends():
            copy.wait_send()

    early = late_odd & jnp.logical_not(held)

    @pl.when(odd)
    def _():
        send_packet(0, range(PIECES), device(packet_to))

    @pl.when(early)
    def _():
        send_packet(1, range(PIECES), device(near_child))

    @pl.when(is_top | right)
    def _():
        sig[0] = jnp.zeros((B, B), F32)
        sig[1] = jnp.zeros((B, B), F32)

    def prepare(i):
        for h in range(2):
            hi, lo = split(af[i, h])
            a_hi[i, :, part(h)] = hi
            a_lo[i, :, part(h)] = lo
            hi_t, lo_t = split(af[i, h].T)
            at_hi[i, part(h), :] = hi_t
            at_lo[i, part(h), :] = lo_t

    def part(h):
        return slice(h * B, (h + 1) * B)

    def put_s(i, row, col, value):
        s_hi[i, part(row), part(col)], s_lo[i, part(row), part(col)] = split(value)

    def three(a, b):
        return mm(a[0], b[0]) + mm(a[0], b[1]) + mm(a[1], b[0])

    def coeff(i, h):
        return a_hi[i, :, part(h)], a_lo[i, :, part(h)]

    def coeff_t(i, h):
        return at_hi[i, part(h), :], at_lo[i, part(h), :]

    def held_s(i, row, col):
        return s_hi[i, part(row), part(col)], s_lo[i, part(row), part(col)]

    def cross_old(i):
        whole = (a_hi[i], a_lo[i])
        wf[i, 0] = -three(whole, (s_hi[i, :, part(0)], s_lo[i, :, part(0)]))

    def partial_new(i):
        tmp[i, 0] = three(coeff(i, 0), held_s(i, 0, 1))

    def partial_sum(i):
        tmp[i, 1] = dpk[i] - three(split(wf[i, 0]), coeff_t(i, 0))

    def cross_new(i):
        wf[i, 1] = -(tmp[i, 0] + three(coeff(i, 1), held_s(i, 1, 1)))

    def newest(i):
        sig[3 + i] = tmp[i, 1] - three(split(wf[i, 1]), coeff_t(i, 1))

    def result(k, src, dst):
        return pltpu.make_async_remote_copy(
            src_ref=src, dst_ref=dst, send_sem=res_send.at[k], recv_sem=res_recv.at[k],
            device_id=device(parent), device_id_type=MESH)

    def sigma_result():
        return [result(i, sig.at[(3, *tri(i))], sig.at[(4, *tri(i))]) for i in range(PIECES)]

    def cross_result():
        own = jnp.where(parent_left, 0, 1)
        return [
            result(PIECES + i, wf.at[0, own, pl.ds(i * Q, Q)], wf.at[1, 0, pl.ds(i * Q, Q)]) for i in range(3)
        ]

    def receive(kinds):
        for k in kinds:
            copy_to(2, k, target(k), target(k)).wait_recv()

            @pl.when(has_next)
            def _():
                copy_to(2, k, target(k), target(k)).start()

    def drain(e, kinds):
        for k in kinds:
            copy_to(e, k, target(k), target(k)).wait_send()

    def drain_packet(e):
        for k, (src, dst) in enumerate(packet_parts()):
            packet(e, k, src, dst, zero_dev).wait_send()

    LAST = range(2 * PIECES, KINDS)

    @pl.when(normal)
    def _():
        dpk[1] = inv_ref[0]
        inverse = split(inv_ref[0])
        for ref, where in ((low_ref, g_half), (up_ref, 1 - g_half)):
            af[1, where] = three(inverse, split(ref[0]))

    @pl.when(odd)
    def _():
        send_packet(0, range(PIECES, PARTS), device(packet_to))

        @pl.when(early)
        def _():
            send_packet(1, range(PIECES, PARTS), device(near_child))

        if n >= 32:
            @pl.when(half_held)
            def _():
                send_packet(1, range(PIECES + 3), device(near_child))

            @pl.when(held)
            def _():
                pl.semaphore_wait(go_sem, 1)

            @pl.when(held & jnp.logical_not(half_held))
            def _():
                send_packet(1, range(PIECES + 3), device(near_child))

            @pl.when(held)
            def _():
                send_packet(1, range(PIECES + 3, PARTS), device(near_child))

        @pl.when(right)
        def _():
            receive(LAST)

        @pl.when(hub)
        def _():
            for k in range(KINDS):
                copy_to(2, k, target(k), target(k)).wait_recv()
                copy_to(2, k, target(k), target(k)).start()
                copy_to(0, k, target(k), target(k), device(t - 6)).start()
            drain(2, range(KINDS))
            drain(0, range(KINDS))

        for copy in sigma_result() + cross_result():
            copy.wait_recv()

        if n >= 32:
            @pl.when(calls)
            def _():
                pl.semaphore_signal(call_sem, inc=1, device_id=device(parent), device_id_type=MESH)

        mirror(sig, 4)
        diag_ref[0] = sig[4]
        cross_ref[0] = wf[1, 0]
        drain_packet(0)

        @pl.when(late_odd)
        def _():
            drain_packet(1)

    @pl.when(is_top)
    def _():
        prepare(1)
        receive(LAST)
        mirror(sig, 2)
        put_s(1, 1, 1, sig[2])
        wf[1, 0] = jnp.zeros((B, B), F32)
        tmp[1, 0] = jnp.zeros((B, B), F32)
        tmp[1, 1] = inv_ref[0]
        cross_new(1)
        send_cross(1)
        newest(1)
        send_newest(0)
        send_newest(1)

    @pl.when(second)
    def _():
        prepare(1)

        def get_packet():
            for k, (_, dst) in enumerate(packet_parts()):
                packet(0, k, dst, dst, zero_dev).wait_recv()

                @pl.when(lower)
                def _():
                    packet(0, k, dst, dst, device(packet_to)).start()

            mirror(dpk, 0)
            prepare(0)

        def go():
            pl.semaphore_signal(go_sem, inc=1, device_id=held_dev, device_id_type=MESH)

        @pl.when(jnp.logical_not(late_packet))
        def _():
            get_packet()

        if n >= 32:
            @pl.when(lower)
            def _():
                go()

        @pl.when(jnp.logical_not(right))
        def _():
            receive(range(2 * PIECES))

        @pl.when(late_packet)
        def _():
            receive(LAST)

            if n >= 32:
                @pl.when(at_start)
                def _():
                    go()

            get_packet()

        def pass_on(kinds):
            @pl.when(forwards)
            def _():
                receive(kinds)

        @pl.when(source & (side == 0))
        def _():
            send_other(0, 0)

        mirror(sig, 0)
        put_s(0, 0, 0, sig[0])
        put_s(0, 1, 0, sig[1])
        put_s(0, 0, 1, sig[1].T)
        pass_on(LAST[:1])
        cross_old(0)
        pass_on(LAST[1:2])
        partial_new(0)
        pass_on(LAST[2:3])
        partial_sum(0)

        def own_early(block):
            s_hi[1, part(0), part(0)], s_lo[1, part(0), part(0)] = held_s(0, block, block)
            put_s(1, 1, 0, wf[0, block])
            put_s(1, 0, 1, wf[0, block].T)
            cross_old(1)

            @pl.when(source)
            def _():
                send_cross(0)

            partial_new(1)
            partial_sum(1)

        @pl.when(side == 0)
        def _():
            own_early(0)

        pass_on(LAST[3:])

        @pl.when(jnp.logical_not(forwards | late_packet))
        def _():
            receive(LAST)

        @pl.when(source & (side == 1))
        def _():
            send_other(0, 2)

        mirror(sig, 2)
        put_s(0, 1, 1, sig[2])
        cross_new(0)
        newest(0)

        @pl.when(source)
        def _():
            send_other(1, 3)

        @pl.when(side == 1)
        def _():
            own_early(1)

        put_s(1, 1, 1, sig[3])
        cross_new(1)

        @pl.when(source)
        def _():
            send_cross(1)

        newest(1)

        @pl.when(source)
        def _():
            send_newest(0)
            send_newest(1)

    @pl.when(normal & even)
    def _():
        diag_ref[0] = sig[4]
        cross_ref[0] = wf[1, g_half]

    @pl.when(source)
    def _():
        drain(0, LAST)
        drain(1, range(PIECES, KINDS))

    @pl.when(second & source)
    def _():
        drain(0, range(2 * PIECES))
        drain(1, range(PIECES))

    @pl.when(has_next)
    def _():
        drain(2, LAST)

    @pl.when(has_next & jnp.logical_not(right))
    def _():
        drain(2, range(2 * PIECES))

    @pl.when(lower)
    def _():
        drain_packet(0)

    if n >= 32:
        @pl.when(lower)
        def _():
            pl.semaphore_wait(call_sem, 1)

    @pl.when(feeds_sigma)
    def _():
        for copy in sigma_result():
            copy.start()

    @pl.when(feeds_cross)
    def _():
        for copy in cross_result():
            copy.start()
        for copy in cross_result():
            copy.wait_send()

    @pl.when(feeds_sigma)
    def _():
        for copy in sigma_result():
            copy.wait_send()


def body(inv_diag, low_coupling, up_coupling):
    n = lax.axis_size("tm")
    B = inv_diag.shape[1]
    vmem = pl.BlockSpec(memory_space=pltpu.VMEM)
    block = jax.ShapeDtypeStruct(inv_diag.shape, F32)
    return pl.pallas_call(
        functools.partial(kernel, n),
        out_shape=(block, block),
        in_specs=[vmem] * 3,
        out_specs=(vmem, vmem),
        scratch_shapes=[
            pltpu.VMEM((5, B, B), F32),
            pltpu.VMEM((2, 2, B, B), F32),
            pltpu.VMEM((2, 2, B, B), F32),
            pltpu.VMEM((2, 2, B, B), F32),
            pltpu.VMEM((2, B, B), F32),
            pltpu.VMEM((2, B, 2 * B), BF16),
            pltpu.VMEM((2, B, 2 * B), BF16),
            pltpu.VMEM((2, 2 * B, B), BF16),
            pltpu.VMEM((2, 2 * B, B), BF16),
            pltpu.VMEM((2, 2 * B, 2 * B), BF16),
            pltpu.VMEM((2, 2 * B, 2 * B), BF16),
            pltpu.SemaphoreType.DMA((3, 3 * PIECES)),
            pltpu.SemaphoreType.DMA((3 * PIECES,)),
            pltpu.SemaphoreType.DMA((2, PIECES + 6)),
            pltpu.SemaphoreType.DMA((PIECES + 6,)),
            pltpu.SemaphoreType.DMA((PIECES + 3,)),
            pltpu.SemaphoreType.DMA((PIECES + 3,)),
            pltpu.SemaphoreType.REGULAR,
            pltpu.SemaphoreType.REGULAR,
        ],
        compiler_params=pltpu.CompilerParams(
            collective_id=0, has_side_effects=True, vmem_limit_bytes=60 * 1024 * 1024
        ),
    )(inv_diag, low_coupling, up_coupling)


def solution(mesh):
    placed = (P("tm", None, None),) * 3
    return jax.shard_map(
        body,
        mesh=mesh,
        in_specs=placed,
        out_specs=(P("tm", None, None), P("tm", None, None)),
        check_vma=False,
    )
```

time: 169 us -> 130 us (0.77)
  the two profiles are of different devices: /device:TPU:88 before, /device:TPU:95 now
where the time goes in v4:
time: 130 us
  Pallas kernels  126 us (97%)
  local copies, waits for them, and re-layouts  2.8 us (2%)
    pallas_call x1, Pallas kernels, body(): pl.pallas_call(functools.partial(kernel, n), out_shape=(block, block), in...  126 us
    unnamed x4, local copies, waits for them, and re-layouts  2.8 us

profile of v4, /device:TPU:95, one launch (start us, length us, event | category | flops | bytes accessed | tf_op | source)
XLA Modules:
  0.0 129.9 jit_solution(4917781252717953009)
XLA Ops:
  0.6 126.4 %shard_map.50 = (f32[1,384,384]{2,1,0:T(8,128)}, f32[1,384,384]{2,1,0:T(8,128)}) custom-call(f32[1,384,384]{2,1,0:T(8,128)} %inv_ref.1, f32[1,384,384]{2,1,0:T(8,128)} %low_ref.1, f32[1,384,384]{2,1,0:T(8,128)} %up_ref.1), custom_call_target="tpu_custom_call" | custom-call | tf_op jit(solution)/shard_map/pallas_call | solution.py:559
  127.1 0.0 copy-start
  127.1 2.0 %copy.7 = f32[1,384,384]{2,1,0:T(8,128)} copy(f32[1,384,384]{2,1,0:T(8,128)} %get-tuple-element.4) | data formatting | bytes 1179648
  129.1 0.0 copy-done
  129.1 0.8 copy.8
Async XLA Ops:
  127.1 2.0 %copy-start = (f32[1,384,384]{2,1,0:T(8,128)S(1)}, f32[1,384,384]{2,1,0:T(8,128)}, u32[]{:S(2)}) copy-start(f32[1,384,384]{2,1,0:T(8,128)} %get-tuple-element.5) | copy-start | bytes 1769476

commit v5 on v4

--- a/solution.py
+++ b/solution.py
@@ -448,21 +448,20 @@
         partial_sum(0)
 
         def own_early(block):
-            s_hi[1, part(0), part(0)], s_lo[1, part(0), part(0)] = held_s(0, block, block)
+            span = pl.ds(pl.multiple_of(block * B, B), B)
+            s_hi[1, part(0), part(0)] = s_hi[0, span, span]
+            s_lo[1, part(0), part(0)] = s_lo[0, span, span]
             put_s(1, 1, 0, wf[0, block])
             put_s(1, 0, 1, wf[0, block].T)
+            partial_new(1)
+
+        ahead = (side == 0) & (s == 1)
+
+        @pl.when(ahead)
+        def _():
+            own_early(0)
             cross_old(1)
-
-            @pl.when(source)
-            def _():
-                send_cross(0)
-
-            partial_new(1)
             partial_sum(1)
-
-        @pl.when(side == 0)
-        def _():
-            own_early(0)
 
         pass_on(LAST[3:])
 
@@ -483,9 +482,9 @@
         def _():
             send_other(1, 3)
 
-        @pl.when(side == 1)
-        def _():
-            own_early(1)
+        @pl.when(jnp.logical_not(ahead))
+        def _():
+            own_early(side)
 
         put_s(1, 1, 1, sig[3])
         cross_new(1)
@@ -493,6 +492,16 @@
         @pl.when(source)
         def _():
             send_cross(1)
+
+        @pl.when(jnp.logical_not(ahead))
+        def _():
+            cross_old(1)
+
+            @pl.when(source)
+            def _():
+                send_cross(0)
+
+            partial_sum(1)
 
         newest(1)
 

time: 130 us -> 124 us (0.954)
  the two profiles are of different devices: /device:TPU:95 before, /device:TPU:22 now
where the time goes in v5:
time: 124 us
  Pallas kernels  120 us (97%)
  local copies, waits for them, and re-layouts  2.8 us (2%)
    pallas_call x1, Pallas kernels, body(): pl.pallas_call(functools.partial(kernel, n), out_shape=(block, block), in...  120 us
    unnamed x4, local copies, waits for them, and re-layouts  2.8 us

profile of v5, /device:TPU:22, one launch (start us, length us, event | category | flops | bytes accessed | tf_op | source)
XLA Modules:
  0.0 123.8 jit_solution(10028999731730740720)
XLA Ops:
  0.6 120.3 %shard_map.50 = (f32[1,384,384]{2,1,0:T(8,128)}, f32[1,384,384]{2,1,0:T(8,128)}) custom-call(f32[1,384,384]{2,1,0:T(8,128)} %inv_ref.1, f32[1,384,384]{2,1,0:T(8,128)} %low_ref.1, f32[1,384,384]{2,1,0:T(8,128)} %up_ref.1), custom_call_target="tpu_custom_call" | custom-call | tf_op jit(solution)/shard_map/pallas_call | solution.py:568
  121.0 0.0 copy-start
  121.0 2.0 %copy.7 = f32[1,384,384]{2,1,0:T(8,128)} copy(f32[1,384,384]{2,1,0:T(8,128)} %get-tuple-element.4) | data formatting | bytes 1179648
  122.9 0.0 copy-done
  123.0 0.8 copy.8
Async XLA Ops:
  121.0 2.0 %copy-start = (f32[1,384,384]{2,1,0:T(8,128)S(1)}, f32[1,384,384]{2,1,0:T(8,128)}, u32[]{:S(2)}) copy-start(f32[1,384,384]{2,1,0:T(8,128)} %get-tuple-element.5) | copy-start | bytes 1769476

commit v6 on v5

--- a/solution.py
+++ b/solution.py
@@ -25,12 +25,18 @@
 
 def kernel(
     n,
-    inv_ref, low_ref, up_ref,
+    inv_hbm, low_hbm, up_hbm,
     diag_ref, cross_ref,
-    sig, wf, tmp, af, dpk, a_hi, a_lo, at_hi, at_lo, s_hi, s_lo,
+    inv_ref, low_ref, up_ref, load_sem, sig, wf, tmp, af, dpk, a_hi, a_lo, at_hi, at_lo, s_hi, s_lo,
     send_sem, recv_sem, pk_send, pk_recv, res_send, res_recv, go_sem, call_sem,
 ):
     B = inv_ref.shape[1]
+    loads = [
+        pltpu.make_async_copy(src, dst, load_sem.at[k])
+        for k, (src, dst) in enumerate(((inv_hbm, inv_ref), (low_hbm, low_ref), (up_hbm, up_ref)))
+    ]
+    for load in loads:
+        load.start()
     Q = B // 3
     H = B // PIECES
     place = lax.axis_index("tm")
@@ -79,7 +85,7 @@
     half_held = t == 5 * n // 16
     calls = held & jnp.logical_not(half_held)
     at_start = t == 3 * n // 8
-    late_packet = (near & parent_left & (2 * s == n // 16) & (t < 3 * n // 4)) | at_start
+    late_packet = (near & parent_left & (2 * s == n // 16) & (t < 3 * n // 4) & (parent != 5 * n // 16)) | at_start
     holder = lower | at_start
 
     bends = n >= 128
@@ -145,6 +151,9 @@
     @pl.when(peers > 0)
     def _():
         pl.semaphore_wait(barrier, peers)
+
+    for load in loads:
+        load.wait()
 
     def tri(i):
         start = i * H // Q * Q
@@ -568,9 +577,13 @@
     return pl.pallas_call(
         functools.partial(kernel, n),
         out_shape=(block, block),
-        in_specs=[vmem] * 3,
+        in_specs=[pl.BlockSpec(memory_space=pl.ANY)] * 3,
         out_specs=(vmem, vmem),
         scratch_shapes=[
+            pltpu.VMEM((1, B, B), F32),
+            pltpu.VMEM((1, B, B), F32),
+            pltpu.VMEM((1, B, B), F32),
+            pltpu.SemaphoreType.DMA((3,)),
             pltpu.VMEM((5, B, B), F32),
             pltpu.VMEM((2, 2, B, B), F32),
             pltpu.VMEM((2, 2, B, B), F32),
@@ -592,7 +605,7 @@
             pltpu.SemaphoreType.REGULAR,
         ],
         compiler_params=pltpu.CompilerParams(
-            collective_id=0, has_side_effects=True, vmem_limit_bytes=60 * 1024 * 1024
+            collective_id=0, has_side_effects=True, vmem_limit_bytes=54_900_000
         ),
     )(inv_diag, low_coupling, up_coupling)
 

time: 124 us -> 122 us (0.984)
    unnamed x4 -> x2, local copies, waits for them, and re-layouts: 2.8 us -> 1.63 us
where the time goes in v6:
time: 122 us
  Pallas kernels  119 us (98%)
  local copies, waits for them, and re-layouts  1.63 us (1%)
    pallas_call x1, Pallas kernels, body(): pl.pallas_call(functools.partial(kernel, n), out_shape=(block, block), in...  119 us

profile of v6, /device:TPU:22, one launch (start us, length us, event | category | flops | bytes accessed | tf_op | source)
XLA Modules:
  0.0 121.6 jit_solution(4710616272742545390)
XLA Ops:
  0.6 119.3 %shard_map.50 = (f32[1,384,384]{2,1,0:T(8,128)S(1)}, f32[1,384,384]{2,1,0:T(8,128)S(1)}) custom-call(f32[1,384,384]{2,1,0:T(8,128)} %inv_hbm.1, f32[1,384,384]{2,1,0:T(8,128)} %low_hbm.1, f32[1,384,384]{2,1,0:T(8,128)} %up_hbm.1), custom_call_target="tpu_custom_call" | custom-call | tf_op jit(solution)/shard_map/pallas_call | solution.py:577
  120.0 0.8 copy.7
  120.8 0.8 copy.8
